TPU v7x, 32 devices: a whole 2x2x4 slice. The times are simulated.
32 devices in a mesh: row: 8 (over z, x), col: 4 (over y, core).
Axes of the slice: x: 2, y: 2, z: 4, core: 2. Of those that a mesh axis runs over, the one named last changes fastest.
Arguments:
- matrix: float32 [16384, 16384], P('row', 'col'), may hold values from -300 to 300, as said below
Outputs:
- trailing: float32 [16384, 16384], P('row', 'col')
- reflectors: float32 [16384, 8], P('row')
Inputs may be any that keep to these rules, and one draw needn't show every extreme that they name: matrix is exactly symmetric.
All inputs are finite; a program needn't handle non-finite values.
Results may differ from a plain program's by a relative error of at most 0.00021.
Values sent between devices are 32-bit elements; how exact they have to be, the bound alone decides.
A program may use at most 128 MiB of HBM per device.

v0:
```python
import jax
import jax.numpy as jnp
from jax import lax
from jax.sharding import PartitionSpec as P

N = 16384
COLS = 8


def from_root(block, axis, source):
    block = jnp.where(lax.axis_index(axis) == source, block, jnp.zeros_like(block))
    return lax.psum(block, axis)


def precise_dot(operand, factor):
    return jnp.dot(
        operand, factor, precision=lax.Precision.HIGHEST, preferred_element_type=jnp.float32
    )


def local(matrix):
    rows_local = matrix.shape[0]
    cols_local = matrix.shape[1]
    row_index = lax.axis_index("row")
    col_index = lax.axis_index("col")
    panel = from_root(matrix[:, :COLS], "col", 0)
    whole_panel = lax.all_gather(panel, "row", axis=0, tiled=True)
    all_ids = jnp.arange(whole_panel.shape[0], dtype=jnp.int32)
    reflect = jnp.zeros((N, COLS), jnp.float32)
    companion = jnp.zeros((N, COLS), jnp.float32)
    for column in range(COLS):
        reflect_rows = lax.dynamic_slice_in_dim(reflect, row_index * rows_local, rows_local, 0)
        companion_rows = lax.dynamic_slice_in_dim(companion, row_index * rows_local, rows_local, 0)
        current = (
            whole_panel[:, column]
            - precise_dot(reflect, companion[column])
            - precise_dot(companion, reflect[column])
        )
        below_whole = jnp.where(all_ids > column, current, 0.0)
        squared = jnp.sum(below_whole * below_whole)
        leading = jnp.sum(jnp.where(all_ids == column + 1, current, 0.0))
        length = jnp.sqrt(squared)
        vector = below_whole + jnp.where(all_ids == column + 1, length, 0.0)
        scaling = 1.0 / (length * (length + leading))
        vector_rows = lax.dynamic_slice_in_dim(vector, row_index * rows_local, rows_local, 0)
        vector_cols = lax.dynamic_slice_in_dim(vector, col_index * cols_local, cols_local, 0)
        weight_comp = precise_dot(companion.T, vector)
        weight_refl = precise_dot(reflect.T, vector)
        row_image = lax.psum(precise_dot(matrix, vector_cols), "col")
        pushed = scaling * (
            row_image
            - precise_dot(reflect_rows, weight_comp)
            - precise_dot(companion_rows, weight_refl)
        )
        inner_product = lax.psum(jnp.sum(pushed * vector_rows), "row")
        update_rows = pushed - 0.5 * scaling * inner_product * vector_rows
        update = lax.all_gather(update_rows, "row", axis=0, tiled=True)
        reflect = reflect.at[:, column].set(vector)
        companion = companion.at[:, column].set(update)
    reflect_rows = lax.dynamic_slice_in_dim(reflect, row_index * rows_local, rows_local, 0)
    companion_rows = lax.dynamic_slice_in_dim(companion, row_index * rows_local, rows_local, 0)
    reflect_cols = lax.dynamic_slice_in_dim(reflect, col_index * cols_local, cols_local, 0)
    companion_cols = lax.dynamic_slice_in_dim(companion, col_index * cols_local, cols_local, 0)
    trailing = (
        matrix
        - precise_dot(reflect_rows, companion_cols.T)
        - precise_dot(companion_rows, reflect_cols.T)
    )
    return (trailing, reflect_rows)


def solution(mesh):
    placed = (P("row", "col"),)
    return jax.shard_map(
        local,
        mesh=mesh,
        in_specs=placed,
        out_specs=(P("row", "col"), P("row", None)),
        check_vma=False,
    )
```

profile of v0, /device:TPU:0, one launch (start us, length us, event | category | flops | bytes accessed | tf_op | source)
XLA Modules:
  0.0 1102.3 jit_solution(3550992194655780149)
XLA Ops:
  7.2 2.3 slice_select_fusion
  10.9 0.7 compare_reduce_fusion.5
  12.3 0.7 compare_reduce_fusion.3
  15.0 35.0 %all-reduce.4.cloned.1.call-done = f32[2048,8]{1,0:T(8,128)} async-done(((f32[2048,8]{1,0:T(8,128)}), f32[2048,8]{1,0:T(8,128)}) %all-reduce.4.cloned.1.call-update) | async-done | bytes 65552 | tf_op jit(solution)/shard_map/psum | solution.py:12
  50.0 161.0 %all_gather.27 = f32[16384,8]{1,0:T(8,128)} all-gather(f32[2048,8]{1,0:T(8,128)} %all-reduce.4.cloned.1.call-done), channel_id=1, replica_groups=mesh['row'=8,'col'=4] {'row'}, dimensions={0}, use_global_device_ids=true | all-gather | bytes 589824 | tf_op jit(solution)/shard_map/all_gather | solution.py:27
  211.0 44.8 %slice_reduce_fusion = (f32[16384]{0:T(1024)S(1)}, f32[16384]{0:T(1024)S(1)}, f32[16384]{0:T(1024)S(1)}, f32[16384]{0:T(1024)S(1)}, f32[16384]{0:T(1024)S(1)}, /...) fusion(f32[16384,8]{1,0:T(8,128)} %all_gather.27), kind=kLoop, calls=%fused_computation.1 | loop fusion | bytes 1048576 | tf_op jit(solution)/shard_map/slice | solution.py:35
  259.0 1.9 fusion.5
  261.2 30.9 %fusion.109 = f32[1,2048]{1,0:T(1,128)S(1)} fusion(f32[4096,1]{0,1:T(1,128)S(1)} %bitcast.330, f32[2048,4096]{1,0:T(8,128)} %param.33), kind=kOutput, calls=%fused_computation.248 | convolution fusion | flops 100663296 | bytes 33579008 | tf_op jit(solution)/shard_map/dot_general | solution.py:16
  292.1 5.8 psum.120
  299.2 21.0 %psum.121 = f32[]{:T(128)} all-reduce(f32[]{:T(128)} %multiply_reduce_fusion.15), channel_id=1, replica_groups=mesh['row'=8,'col'=4] {'row'}, use_global_device_ids=true, to_apply=%region_7.8 | all-reduce | flops 1 | bytes 8 | tf_op jit(solution)/shard_map/psum | solution.py:55
  320.9 30.5 %all_gather.28 = f32[16384]{0:T(1024)S(1)} all-gather(f32[2048]{0:T(1024)S(1)} %multiply_subtract_fusion.7), channel_id=1, replica_groups=mesh['row'=8,'col'=4] {'row'}, dimensions={0}, use_global_device_ids=true | all-gather | bytes 73728 | tf_op jit(solution)/shard_map/all_gather | solution.py:57
  355.4 1.2 convolution_bitcast_fusion.12
  356.6 1.2 convolution_bitcast_fusion.13
  359.1 30.9 %fusion.110 = f32[1,2048]{1,0:T(1,128)S(1)} fusion(f32[4096,1]{0,1:T(1,128)S(1)} %bitcast.323, f32[2048,4096]{1,0:T(8,128)} %param.33), kind=kOutput, calls=%fused_computation.249 | convolution fusion | flops 100663296 | bytes 33579008 | tf_op jit(solution)/shard_map/dot_general | solution.py:16
  390.0 5.8 psum.122
  396.4 17.7 %psum.123 = f32[]{:T(128)} all-reduce(f32[]{:T(128)} %get-tuple-element.236), channel_id=1, replica_groups=mesh['row'=8,'col'=4] {'row'}, use_global_device_ids=true, to_apply=%region_13.14 | all-reduce | flops 1 | bytes 8 | tf_op jit(solution)/shard_map/psum | solution.py:55
  414.8 30.5 %all_gather.29 = f32[16384]{0:T(1024)S(1)} all-gather(f32[2048]{0:T(1024)S(1)} %multiply_subtract_fusion.6), channel_id=1, replica_groups=mesh['row'=8,'col'=4] {'row'}, dimensions={0}, use_global_device_ids=true | all-gather | bytes 73728 | tf_op jit(solution)/shard_map/all_gather | solution.py:57
  446.1 1.0 scatter.59
  450.3 1.2 convolution_bitcast_fusion.10
  451.6 1.2 convolution_bitcast_fusion.11
  453.9 30.7 %fusion.111 = f32[1,2048]{1,0:T(1,128)S(1)} fusion(f32[4096,1]{0,1:T(1,128)S(1)} %bitcast.325, f32[2048,4096]{1,0:T(8,128)} %param.33), kind=kOutput, calls=%fused_computation.250 | convolution fusion | flops 100663296 | bytes 33579008 | tf_op jit(solution)/shard_map/dot_general | solution.py:16
  484.6 5.8 psum.124
  491.0 19.7 %psum.125 = f32[]{:T(128)} all-reduce(f32[]{:T(128)} %get-tuple-element.233), channel_id=1, replica_groups=mesh['row'=8,'col'=4] {'row'}, use_global_device_ids=true, to_apply=%region_19.20 | all-reduce | flops 1 | bytes 8 | tf_op jit(solution)/shard_map/psum | solution.py:55
  511.4 30.5 %all_gather.30 = f32[16384]{0:T(1024)S(1)} all-gather(f32[2048]{0:T(1024)S(1)} %multiply_subtract_fusion.5), channel_id=1, replica_groups=mesh['row'=8,'col'=4] {'row'}, dimensions={0}, use_global_device_ids=true | all-gather | bytes 73728 | tf_op jit(solution)/shard_map/all_gather | solution.py:57
  542.0 0.7 broadcast_select_fusion.9
  542.7 0.7 broadcast_select_fusion.8
  547.4 1.2 convolution_bitcast_fusion.8
  548.7 1.2 convolution_bitcast_fusion.9
  551.0 30.7 %fusion.112 = f32[1,2048]{1,0:T(1,128)S(1)} fusion(f32[4096,1]{0,1:T(1,128)S(1)} %bitcast.326, f32[2048,4096]{1,0:T(8,128)} %param.33), kind=kOutput, calls=%fused_computation.251 | convolution fusion | flops 100663296 | bytes 33579008 | tf_op jit(solution)/shard_map/dot_general | solution.py:16
  581.7 5.8 psum.126
  588.1 17.8 %psum.127 = f32[]{:T(128)} all-reduce(f32[]{:T(128)} %get-tuple-element.230), channel_id=1, replica_groups=mesh['row'=8,'col'=4] {'row'}, use_global_device_ids=true, to_apply=%region_25.26 | all-reduce | flops 1 | bytes 8 | tf_op jit(solution)/shard_map/psum | solution.py:55
  606.5 30.5 %all_gather.31 = f32[16384]{0:T(1024)S(1)} all-gather(f32[2048]{0:T(1024)S(1)} %multiply_subtract_fusion.4), channel_id=1, replica_groups=mesh['row'=8,'col'=4] {'row'}, dimensions={0}, use_global_device_ids=true | all-gather | bytes 73728 | tf_op jit(solution)/shard_map/all_gather | solution.py:57
  637.1 0.8 broadcast_select_fusion.7
  637.8 0.8 broadcast_select_fusion.6
  642.7 1.2 convolution_bitcast_fusion.6
  643.9 1.2 convolution_bitcast_fusion.7
  646.3 30.7 %fusion.113 = f32[1,2048]{1,0:T(1,128)S(1)} fusion(f32[4096,1]{0,1:T(1,128)S(1)} %bitcast.327, f32[2048,4096]{1,0:T(8,128)} %param.33), kind=kOutput, calls=%fused_computation.252 | convolution fusion | flops 100663296 | bytes 33579008 | tf_op jit(solution)/shard_map/dot_general | solution.py:16
  676.9 5.8 psum.128
  683.3 19.7 %psum.129 = f32[]{:T(128)} all-reduce(f32[]{:T(128)} %get-tuple-element.227), channel_id=1, replica_groups=mesh['row'=8,'col'=4] {'row'}, use_global_device_ids=true, to_apply=%region_31.32 | all-reduce | flops 1 | bytes 8 | tf_op jit(solution)/shard_map/psum | solution.py:55
  703.7 30.5 %all_gather.32 = f32[16384]{0:T(1024)S(1)} all-gather(f32[2048]{0:T(1024)S(1)} %multiply_subtract_fusion.3), channel_id=1, replica_groups=mesh['row'=8,'col'=4] {'row'}, dimensions={0}, use_global_device_ids=true | all-gather | bytes 73728 | tf_op jit(solution)/shard_map/all_gather | solution.py:57
  735.0 0.7 broadcast_select_fusion.4
  735.7 0.9 scatter.69
  739.9 1.2 convolution_bitcast_fusion.4
  741.2 1.2 convolution_bitcast_fusion.5
  743.5 30.7 %fusion.114 = f32[1,2048]{1,0:T(1,128)S(1)} fusion(f32[4096,1]{0,1:T(1,128)S(1)} %bitcast.328, f32[2048,4096]{1,0:T(8,128)} %param.33), kind=kOutput, calls=%fused_computation.253 | convolution fusion | flops 100663296 | bytes 33579008 | tf_op jit(solution)/shard_map/dot_general | solution.py:16
  774.2 5.9 psum.130
  780.7 17.7 %psum.131 = f32[]{:T(128)} all-reduce(f32[]{:T(128)} %get-tuple-element.224), channel_id=1, replica_groups=mesh['row'=8,'col'=4] {'row'}, use_global_device_ids=true, to_apply=%region_37.38 | all-reduce | flops 1 | bytes 8 | tf_op jit(solution)/shard_map/psum | solution.py:55
  799.1 30.5 %all_gather.33 = f32[16384]{0:T(1024)S(1)} all-gather(f32[2048]{0:T(1024)S(1)} %multiply_subtract_fusion.2), channel_id=1, replica_groups=mesh['row'=8,'col'=4] {'row'}, dimensions={0}, use_global_device_ids=true | all-gather | bytes 73728 | tf_op jit(solution)/shard_map/all_gather | solution.py:57
  830.4 0.7 broadcast_select_fusion.2
  835.1 1.2 convolution_bitcast_fusion.2
  836.3 1.2 convolution_bitcast_fusion.3
  838.7 30.7 %fusion.115 = f32[1,2048]{1,0:T(1,128)S(1)} fusion(f32[4096,1]{0,1:T(1,128)S(1)} %bitcast.329, f32[2048,4096]{1,0:T(8,128)} %param.33), kind=kOutput, calls=%fused_computation.254 | convolution fusion | flops 100663296 | bytes 33579008 | tf_op jit(solution)/shard_map/dot_general | solution.py:16
  869.4 5.9 psum.132
  875.9 19.7 %psum.133 = f32[]{:T(128)} all-reduce(f32[]{:T(128)} %get-tuple-element.221), channel_id=1, replica_groups=mesh['row'=8,'col'=4] {'row'}, use_global_device_ids=true, to_apply=%region_42.43 | all-reduce | flops 1 | bytes 8 | tf_op jit(solution)/shard_map/psum | solution.py:55
  896.3 30.5 %all_gather.34 = f32[16384]{0:T(1024)S(1)} all-gather(f32[2048]{0:T(1024)S(1)} %multiply_subtract_fusion.1), channel_id=1, replica_groups=mesh['row'=8,'col'=4] {'row'}, dimensions={0}, use_global_device_ids=true | all-gather | bytes 73728 | tf_op jit(solution)/shard_map/all_gather | solution.py:57
  932.2 1.2 convolution_bitcast_fusion
  933.4 1.2 convolution_bitcast_fusion.1
  935.8 30.7 %fusion.116 = f32[1,2048]{1,0:T(1,128)S(1)} fusion(f32[4096,1]{0,1:T(1,128)S(1)} %bitcast.324, f32[2048,4096]{1,0:T(8,128)} %param.33), kind=kOutput, calls=%fused_computation.255 | convolution fusion | flops 100663296 | bytes 33579008 | tf_op jit(solution)/shard_map/dot_general | solution.py:16
  966.5 5.9 psum.134
  973.5 17.8 %psum.135 = f32[]{:T(128)} all-reduce(f32[]{:T(128)} %get-tuple-element.218), channel_id=1, replica_groups=mesh['row'=8,'col'=4] {'row'}, use_global_device_ids=true, to_apply=%region_47.48 | all-reduce | flops 1 | bytes 8 | tf_op jit(solution)/shard_map/psum | solution.py:55
  991.9 30.5 %all_gather.35 = f32[16384]{0:T(1024)S(1)} all-gather(f32[2048]{0:T(1024)S(1)} %multiply_subtract_fusion), channel_id=1, replica_groups=mesh['row'=8,'col'=4] {'row'}, dimensions={0}, use_global_device_ids=true | all-gather | bytes 73728 | tf_op jit(solution)/shard_map/all_gather | solution.py:57
  1022.4 0.7 scatter.79
  1023.2 30.3 %fusion.20 = f32[2048,4096]{1,0:T(8,128)} fusion(f32[2048,8]{0,1:T(8,128)S(1)} %constant_dynamic-slice_fusion, f32[16384,8]{0,1:T(8,128)S(1)} %scatter.79, s32[]{:T(128)S(6)} %select_n.125), kind=kOutput, calls=%fused_computation.51 | convolution fusion | flops 805306368 | bytes 33751044 | tf_op jit(solution)/shard_map/dot_general | solution.py:16
  1053.5 41.4 %subtract_subtract_fusion = f32[2048,4096]{1,0:T(8,128)} fusion(f32[2048,4096]{1,0:T(8,128)} %param.33, f32[2048,4096]{1,0:T(8,128)} %fusion.20, f32[16384,8]{0,1:T(8,128)S(1)} %scatter.76, s32[]{:T(128)S(6)} %select_n.125, f32[16384,8]{0,1:T(8,128)S(1)} %scatter.79, s32[]{:T(128)S(6)} %select_n.126), kind=kOutput, calls=%fused_computation | convolution fusion | flops 822083584 | bytes 100859912 | tf_op jit(solution)/shard_map/dot_general | solution.py:16
  (114 shorter events, 40.2 us)
Async XLA Ops:
  7.2 42.8 %all-reduce.4.cloned.1.call-start = ((), (), s32[]{:S(2)}) async-start(), calls=%async_computation | async-start | bytes 2097152 | tf_op jit(solution)/shard_map/psum | solution.py:12
  1023.2 71.7 %copy-start = (f32[2048,8]{0,1:T(8,128)}, f32[2048,8]{0,1:T(8,128)S(1)}, u32[]{:S(2)}) copy-start(f32[2048,8]{0,1:T(8,128)S(1)} %constant_dynamic-slice_fusion) | copy-start | bytes 196612
Sparse Core Ops, SparseCore 0:
  10.9 39.0 all-reduce.3
where the time goes:
time: 1110 us; the launch traced here: 1100 us
  blocking collectives  603 us (54%)
  matrix products  348 us (31%)
  local copies, waits for them, and re-layouts  57.5 us (5%)
  waiting for transfers between devices  35 us (3%)
  between operations  31.6 us (3%)
  other arithmetic  27.5 us (2%)
    dot_general x53, matrix products, precise_dot(): jnp.dot(operand, factor, precision=lax.Precision.HIGHEST, preferred_eleme...  348 us
    all_gather x8, blocking collectives, local(): update = lax.all_gather(update_rows, 'row', axis=0, tiled=True)  244 us
    all_gather x1, blocking collectives, local(): whole_panel = lax.all_gather(panel, 'row', axis=0, tiled=True)  161 us
    psum x8, blocking collectives, local(): inner_product = lax.psum(jnp.sum(pushed * vector_rows), 'row')  151 us
    psum x8, blocking collectives, local(): row_image = lax.psum(precise_dot(matrix, vector_cols), 'col')  46.5 us
    slice x1, local copies, waits for them, and re-layouts, local(): whole_panel[:, column] - precise_dot(reflect, companion[column])  44.8 us
    psum x1, waiting for transfers between devices, from_root(): return lax.psum(block, axis)  35 us
  transfers between devices with their start and end apart: 1, of which 1 were waited for; matrix products, arithmetic and copies ran while one was open for 0% of the time, Pallas kernels for 0%

commit v1 on v0

--- a/solution.py
+++ b/solution.py
@@ -24,7 +24,12 @@
     row_index = lax.axis_index("row")
     col_index = lax.axis_index("col")
     panel = from_root(matrix[:, :COLS], "col", 0)
-    whole_panel = lax.all_gather(panel, "row", axis=0, tiled=True)
+    ring = [panel]
+    for hop in range(7):
+        ring.append(lax.ppermute(ring[-1], "row", [(dev, (dev + 1) % 8) for dev in range(8)]))
+    whole_panel = jnp.roll(
+        jnp.concatenate(ring[::-1], axis=0), (lax.axis_index("row") + 1) * ring[0].shape[0], axis=0
+    )
     all_ids = jnp.arange(whole_panel.shape[0], dtype=jnp.int32)
     reflect = jnp.zeros((N, COLS), jnp.float32)
     companion = jnp.zeros((N, COLS), jnp.float32)

time: 1110 us -> 952 us (0.86)
  blocking collectives: 603 us -> 444 us
  waiting for transfers between devices: 35 us -> 78.4 us
  local copies, waits for them, and re-layouts: 57.5 us -> 15.3 us
    all_gather x1 -> x0, blocking collectives: 161 us -> none  [local(): whole_panel = lax.all_gather(panel, 'row', axis=0, tiled=True)]
    slice x1, local copies, waits for them, and re-layouts: 44.8 us -> 1.01 us  [local(): whole_panel[:, column] - precise_dot(reflect, companion[column])]
    ppermute x0 -> x7, waiting for transfers between devices: none -> 42.8 us  [local(): lax.ppermute(ring[-1], 'row', [(dev, (dev + 1) % 8) for dev in range(8)])]
  transfers between devices with their start and end apart: 1 -> 8, of which waited for: 1 -> 8; matrix products, arithmetic and copies ran while one was open for 0% -> 1% of each run, Pallas kernels for 0% -> 0%
where the time goes in v1:
time: 952 us; the launch traced here: 944 us
  blocking collectives  444 us (47%)
  matrix products  347 us (36%)
  waiting for transfers between devices  78.4 us (8%)
  between operations  31.8 us (3%)
  other arithmetic  25.7 us (3%)
  local copies, waits for them, and re-layouts  15.3 us (2%)
    dot_general x53, matrix products, precise_dot(): jnp.dot(operand, factor, precision=lax.Precision.HIGHEST, preferred_eleme...  347 us
    all_gather x8, blocking collectives, local(): update = lax.all_gather(update_rows, 'row', axis=0, tiled=True)  246 us
    psum x8, blocking collectives, local(): inner_product = lax.psum(jnp.sum(pushed * vector_rows), 'row')  151 us
    psum x8, blocking collectives, local(): row_image = lax.psum(precise_dot(matrix, vector_cols), 'col')  46.9 us
    ppermute x7, waiting for transfers between devices, local(): lax.ppermute(ring[-1], 'row', [(dev, (dev + 1) % 8) for dev in range(8)])  42.8 us
    psum x1, waiting for transfers between devices, from_root(): return lax.psum(block, axis)  35.7 us
  transfers between devices with their start and end apart: 8, of which 8 were waited for; matrix products, arithmetic and copies ran while one was open for 1% of the time, Pallas kernels for 0%

profile of v1, /device:TPU:0, one launch (start us, length us, event | category | flops | bytes accessed | tf_op | source)
XLA Modules:
  0.0 944.1 jit_solution(16564251371993421541)
XLA Ops:
  7.2 1.3 slice.327
  9.5 35.7 %all-reduce.4.cloned.1.call-done = f32[2048,8]{0,1:T(8,128)} async-done(((f32[2048,8]{0,1:T(8,128)}), f32[2048,8]{0,1:T(8,128)}) %all-reduce.4.cloned.1.call-update) | async-done | bytes 65552 | tf_op jit(solution)/shard_map/psum | solution.py:12
  45.1 1.5 collective-permute-start
  46.6 5.7 collective-permute-done
  52.3 7.0 collective-permute-done.1
  59.3 7.0 collective-permute-done.2
  66.2 7.6 collective-permute-done.3
  73.8 7.0 collective-permute-done.4
  80.8 7.0 collective-permute-done.5
  93.1 1.6 collective-permute-done.6
  94.8 0.8 constant_dynamic-update-slice_fusion.8
  95.8 0.8 constant_dynamic-update-slice_fusion
  96.6 1.0 fusion.109
  101.1 1.9 fusion.5
  103.2 30.7 %fusion.110 = f32[1,2048]{1,0:T(1,128)S(1)} fusion(f32[4096,1]{0,1:T(1,128)S(1)} %bitcast.347, f32[2048,4096]{1,0:T(8,128)} %param.33), kind=kOutput, calls=%fused_computation.258 | convolution fusion | flops 100663296 | bytes 33579008 | tf_op jit(solution)/shard_map/dot_general | solution.py:16
  133.9 5.9 psum.120
  141.1 20.8 %psum.121 = f32[]{:T(128)} all-reduce(f32[]{:T(128)} %multiply_reduce_fusion.15), channel_id=1, replica_groups=mesh['row'=8,'col'=4] {'row'}, use_global_device_ids=true, to_apply=%region_7.8 | all-reduce | flops 1 | bytes 8 | tf_op jit(solution)/shard_map/psum | solution.py:60
  162.6 30.7 %all_gather.24 = f32[16384]{0:T(1024)S(1)} all-gather(f32[2048]{0:T(1024)S(1)} %multiply_subtract_fusion.7), channel_id=1, replica_groups=mesh['row'=8,'col'=4] {'row'}, dimensions={0}, use_global_device_ids=true | all-gather | bytes 73728 | tf_op jit(solution)/shard_map/all_gather | solution.py:62
  197.2 1.2 convolution_bitcast_fusion.12
  198.5 1.2 convolution_bitcast_fusion.13
  200.9 30.7 %fusion.111 = f32[1,2048]{1,0:T(1,128)S(1)} fusion(f32[4096,1]{0,1:T(1,128)S(1)} %bitcast.340, f32[2048,4096]{1,0:T(8,128)} %param.33), kind=kOutput, calls=%fused_computation.259 | convolution fusion | flops 100663296 | bytes 33579008 | tf_op jit(solution)/shard_map/dot_general | solution.py:16
  231.6 5.9 psum.122
  238.1 17.7 %psum.123 = f32[]{:T(128)} all-reduce(f32[]{:T(128)} %get-tuple-element.228), channel_id=1, replica_groups=mesh['row'=8,'col'=4] {'row'}, use_global_device_ids=true, to_apply=%region_13.14 | all-reduce | flops 1 | bytes 8 | tf_op jit(solution)/shard_map/psum | solution.py:60
  256.5 30.9 %all_gather.25 = f32[16384]{0:T(1024)S(1)} all-gather(f32[2048]{0:T(1024)S(1)} %multiply_subtract_fusion.6), channel_id=1, replica_groups=mesh['row'=8,'col'=4] {'row'}, dimensions={0}, use_global_device_ids=true | all-gather | bytes 73728 | tf_op jit(solution)/shard_map/all_gather | solution.py:62
  291.9 1.2 convolution_bitcast_fusion.10
  293.1 1.2 convolution_bitcast_fusion.11
  295.5 30.7 %fusion.112 = f32[1,2048]{1,0:T(1,128)S(1)} fusion(f32[4096,1]{0,1:T(1,128)S(1)} %bitcast.342, f32[2048,4096]{1,0:T(8,128)} %param.33), kind=kOutput, calls=%fused_computation.260 | convolution fusion | flops 100663296 | bytes 33579008 | tf_op jit(solution)/shard_map/dot_general | solution.py:16
  326.2 5.9 psum.124
  332.7 19.7 %psum.125 = f32[]{:T(128)} all-reduce(f32[]{:T(128)} %get-tuple-element.225), channel_id=1, replica_groups=mesh['row'=8,'col'=4] {'row'}, use_global_device_ids=true, to_apply=%region_19.20 | all-reduce | flops 1 | bytes 8 | tf_op jit(solution)/shard_map/psum | solution.py:60
  353.1 30.7 %all_gather.26 = f32[16384]{0:T(1024)S(1)} all-gather(f32[2048]{0:T(1024)S(1)} %multiply_subtract_fusion.5), channel_id=1, replica_groups=mesh['row'=8,'col'=4] {'row'}, dimensions={0}, use_global_device_ids=true | all-gather | bytes 73728 | tf_op jit(solution)/shard_map/all_gather | solution.py:62
  389.1 1.2 convolution_bitcast_fusion.8
  390.3 1.2 convolution_bitcast_fusion.9
  392.7 30.7 %fusion.113 = f32[1,2048]{1,0:T(1,128)S(1)} fusion(f32[4096,1]{0,1:T(1,128)S(1)} %bitcast.343, f32[2048,4096]{1,0:T(8,128)} %param.33), kind=kOutput, calls=%fused_computation.261 | convolution fusion | flops 100663296 | bytes 33579008 | tf_op jit(solution)/shard_map/dot_general | solution.py:16
  423.3 5.9 psum.126
  429.8 17.8 %psum.127 = f32[]{:T(128)} all-reduce(f32[]{:T(128)} %get-tuple-element.222), channel_id=1, replica_groups=mesh['row'=8,'col'=4] {'row'}, use_global_device_ids=true, to_apply=%region_25.26 | all-reduce | flops 1 | bytes 8 | tf_op jit(solution)/shard_map/psum | solution.py:60
  448.3 30.7 %all_gather.27 = f32[16384]{0:T(1024)S(1)} all-gather(f32[2048]{0:T(1024)S(1)} %multiply_subtract_fusion.4), channel_id=1, replica_groups=mesh['row'=8,'col'=4] {'row'}, dimensions={0}, use_global_device_ids=true | all-gather | bytes 73728 | tf_op jit(solution)/shard_map/all_gather | solution.py:62
  484.1 1.2 convolution_bitcast_fusion.6
  485.4 1.2 convolution_bitcast_fusion.7
  487.7 30.7 %fusion.114 = f32[1,2048]{1,0:T(1,128)S(1)} fusion(f32[4096,1]{0,1:T(1,128)S(1)} %bitcast.344, f32[2048,4096]{1,0:T(8,128)} %param.33), kind=kOutput, calls=%fused_computation.262 | convolution fusion | flops 100663296 | bytes 33579008 | tf_op jit(solution)/shard_map/dot_general | solution.py:16
  518.4 5.9 psum.128
  524.9 19.7 %psum.129 = f32[]{:T(128)} all-reduce(f32[]{:T(128)} %get-tuple-element.219), channel_id=1, replica_groups=mesh['row'=8,'col'=4] {'row'}, use_global_device_ids=true, to_apply=%region_31.32 | all-reduce | flops 1 | bytes 8 | tf_op jit(solution)/shard_map/psum | solution.py:60
  545.3 30.9 %all_gather.28 = f32[16384]{0:T(1024)S(1)} all-gather(f32[2048]{0:T(1024)S(1)} %multiply_subtract_fusion.3), channel_id=1, replica_groups=mesh['row'=8,'col'=4] {'row'}, dimensions={0}, use_global_device_ids=true | all-gather | bytes 73728 | tf_op jit(solution)/shard_map/all_gather | solution.py:62
  577.0 0.8 broadcast_select_fusion.4
  581.7 1.2 convolution_bitcast_fusion.4
  582.9 1.2 convolution_bitcast_fusion.5
  585.3 30.7 %fusion.115 = f32[1,2048]{1,0:T(1,128)S(1)} fusion(f32[4096,1]{0,1:T(1,128)S(1)} %bitcast.345, f32[2048,4096]{1,0:T(8,128)} %param.33), kind=kOutput, calls=%fused_computation.263 | convolution fusion | flops 100663296 | bytes 33579008 | tf_op jit(solution)/shard_map/dot_general | solution.py:16
  616.0 5.9 psum.130
  622.4 17.8 %psum.131 = f32[]{:T(128)} all-reduce(f32[]{:T(128)} %get-tuple-element.216), channel_id=1, replica_groups=mesh['row'=8,'col'=4] {'row'}, use_global_device_ids=true, to_apply=%region_37.38 | all-reduce | flops 1 | bytes 8 | tf_op jit(solution)/shard_map/psum | solution.py:60
  640.9 30.7 %all_gather.29 = f32[16384]{0:T(1024)S(1)} all-gather(f32[2048]{0:T(1024)S(1)} %multiply_subtract_fusion.2), channel_id=1, replica_groups=mesh['row'=8,'col'=4] {'row'}, dimensions={0}, use_global_device_ids=true | all-gather | bytes 73728 | tf_op jit(solution)/shard_map/all_gather | solution.py:62
  676.7 1.2 convolution_bitcast_fusion.2
  677.9 1.2 convolution_bitcast_fusion.3
  680.3 30.7 %fusion.116 = f32[1,2048]{1,0:T(1,128)S(1)} fusion(f32[4096,1]{0,1:T(1,128)S(1)} %bitcast.346, f32[2048,4096]{1,0:T(8,128)} %param.33), kind=kOutput, calls=%fused_computation.264 | convolution fusion | flops 100663296 | bytes 33579008 | tf_op jit(solution)/shard_map/dot_general | solution.py:16
  711.0 5.9 psum.132
  717.5 19.7 %psum.133 = f32[]{:T(128)} all-reduce(f32[]{:T(128)} %get-tuple-element.213), channel_id=1, replica_groups=mesh['row'=8,'col'=4] {'row'}, use_global_device_ids=true, to_apply=%region_42.43 | all-reduce | flops 1 | bytes 8 | tf_op jit(solution)/shard_map/psum | solution.py:60
  737.9 30.7 %all_gather.30 = f32[16384]{0:T(1024)S(1)} all-gather(f32[2048]{0:T(1024)S(1)} %multiply_subtract_fusion.1), channel_id=1, replica_groups=mesh['row'=8,'col'=4] {'row'}, dimensions={0}, use_global_device_ids=true | all-gather | bytes 73728 | tf_op jit(solution)/shard_map/all_gather | solution.py:62
  769.4 0.8 broadcast_select_fusion
  774.0 1.2 convolution_bitcast_fusion
  775.2 1.2 convolution_bitcast_fusion.1
  777.6 30.7 %fusion.117 = f32[1,2048]{1,0:T(1,128)S(1)} fusion(f32[4096,1]{0,1:T(1,128)S(1)} %bitcast.341, f32[2048,4096]{1,0:T(8,128)} %param.33), kind=kOutput, calls=%fused_computation.265 | convolution fusion | flops 100663296 | bytes 33579008 | tf_op jit(solution)/shard_map/dot_general | solution.py:16
  808.3 5.9 psum.134
  815.3 17.8 %psum.135 = f32[]{:T(128)} all-reduce(f32[]{:T(128)} %get-tuple-element.210), channel_id=1, replica_groups=mesh['row'=8,'col'=4] {'row'}, use_global_device_ids=true, to_apply=%region_47.48 | all-reduce | flops 1 | bytes 8 | tf_op jit(solution)/shard_map/psum | solution.py:60
  833.7 30.8 %all_gather.31 = f32[16384]{0:T(1024)S(1)} all-gather(f32[2048]{0:T(1024)S(1)} %multiply_subtract_fusion), channel_id=1, replica_groups=mesh['row'=8,'col'=4] {'row'}, dimensions={0}, use_global_device_ids=true | all-gather | bytes 73728 | tf_op jit(solution)/shard_map/all_gather | solution.py:62
  865.0 30.3 %fusion.20 = f32[2048,4096]{1,0:T(8,128)} fusion(f32[2048,8]{0,1:T(8,128)S(1)} %constant_dynamic-slice_fusion.1, f32[16384,8]{0,1:T(8,128)S(1)} %scatter.79, s32[]{:T(128)S(6)} %select_n.140), kind=kOutput, calls=%fused_computation.42 | convolution fusion | flops 805306368 | bytes 33751044 | tf_op jit(solution)/shard_map/dot_general | solution.py:16
  895.4 41.4 %subtract_subtract_fusion = f32[2048,4096]{1,0:T(8,128)} fusion(f32[2048,4096]{1,0:T(8,128)} %param.33, f32[2048,4096]{1,0:T(8,128)} %fusion.20, f32[16384,8]{0,1:T(8,128)S(1)} %scatter.76, s32[]{:T(128)S(6)} %select_n.140, f32[16384,8]{0,1:T(8,128)S(1)} %scatter.79, s32[]{:T(128)S(6)} %select_n.141), kind=kOutput, calls=%fused_computation | convolution fusion | flops 822083584 | bytes 100859912 | tf_op jit(solution)/shard_map/dot_general | solution.py:16
  (145 shorter events, 46.0 us)
Async XLA Ops:
  7.2 38.0 %all-reduce.4.cloned.1.call-start = ((), (), s32[]{:S(2)}) async-start(), calls=%async_computation | async-start | bytes 131072 | tf_op jit(solution)/shard_map/psum | solution.py:12
  45.1 7.2 collective-permute-start
  52.3 7.0 collective-permute-start.1
  59.3 7.0 collective-permute-start.2
  66.2 7.6 collective-permute-start.3
  73.8 7.0 collective-permute-start.4
  80.8 7.0 collective-permute-start.5
  87.8 7.0 collective-permute-start.6
  865.0 71.7 %copy-start = (f32[2048,8]{0,1:T(8,128)}, f32[2048,8]{0,1:T(8,128)S(1)}, u32[]{:S(2)}) copy-start(f32[2048,8]{0,1:T(8,128)S(1)} %constant_dynamic-slice_fusion.1) | copy-start | bytes 196612
Sparse Core Ops, SparseCore 0:
  10.9 34.2 all-reduce.3
